TPU v7x, 512 devices: a whole 4x4x16 slice. The times are simulated.
512 devices in a mesh: fib: 16 (over y, x), blk: 32 (over z, core).
Axes of the slice: x: 4, y: 4, z: 16, core: 2. Of those that a mesh axis runs over, the one named last changes fastest.
Arguments:
- field_data: float32 [33, 64, 512, 256], P(None, 'blk', 'fib'), may hold values from -120 to 120
- start_block: float32 [512, 64], replicated, may hold values from -6 to 6
Outputs:
- core_out: float32 [33, 64, 64, 256], P(None, 'blk', 'fib')
All inputs are finite; a program needn't handle non-finite values.
Results may differ from a plain program's by a relative error of at most 0.00013.
Values sent between devices are 32-bit elements; how exact they have to be, the bound alone decides.
A program may use at most 192 MiB of HBM per device.

v0:
```python
import jax
import jax.numpy as jnp
from jax import lax
from jax.sharding import PartitionSpec as P


def shards(field_data, start_block):
    highest = lax.Precision.HIGHEST
    received = lax.all_to_all(field_data, "fib", split_axis=3, concat_axis=2, tiled=True)
    width_x = received.shape[2]
    unfolded = jnp.transpose(received, (0, 1, 3, 2)).reshape(-1, width_x)
    contract_rows = (((0,), (0,)), ((), ()))
    local_gram = lax.dot_general(unfolded, unfolded, contract_rows, precision=highest)
    gram_total = lax.psum(local_gram, ("fib", "blk"))
    raw_basis = jnp.dot(gram_total, start_block, precision=highest)
    inner_block = jnp.dot(raw_basis.T, raw_basis, precision=highest)
    lower_factor = jnp.linalg.cholesky(inner_block)
    basis_cols = jax.scipy.linalg.solve_triangular(lower_factor, raw_basis.T, lower=True).T
    core_local = jnp.einsum("szxy,xr->szry", received, basis_cols, precision=highest)
    return lax.all_to_all(core_local, "fib", split_axis=2, concat_axis=3, tiled=True)


def solution(mesh):
    in_specs = (P(None, "blk", "fib", None), P())
    out_specs = P(None, "blk", "fib", None)
    return jax.shard_map(shards, mesh=mesh, in_specs=in_specs, out_specs=out_specs, check_vma=False)
```

profile of v0, /device:TPU:1, one launch (start us, length us, event | category | flops | bytes accessed | tf_op | source)
XLA Modules:
  0.0 619.4 jit_solution(7491580162648552195)
XLA Ops:
  6.5 0.0 copy-start
  6.5 0.0 all-reduce.2.cloned.1.call-start
  6.5 8.7 %copy.13 = f32[33,2,32,256]{0,2,1,3:T(8,128)} copy(f32[33,2,32,256]{3,2,1,0:T(8,128)} %param.2) | data formatting | bytes 4325376 | tf_op args[0]
  15.2 10.1 %reshape.13 = f32[16,1,33792]{2,1,0:T(1,128)S(1)} reshape(f32[256,2,32,33]{3,2,1,0:T(8,128)} %bitcast.45) | data formatting | bytes 4325376
  25.3 34.1 %all_to_all.36 = f32[16,1,33792]{2,1,0:T(1,128)} all-to-all(f32[16,1,33792]{2,1,0:T(1,128)S(1)} %reshape.13), channel_id=1, replica_groups=mesh['fib'=16,'blk'=32] {'fib'}, dimensions={0} | all-to-all | bytes 4325376 | tf_op jit(solution)/shard_map/all_to_all | solution.py:9
  59.4 0.5 broadcast.53
  59.9 7.4 %reduce.6 = f32[16,33792]{1,0:T(8,128)S(1)} reduce(f32[16,1,33792]{2,1,0:T(1,128)} %all_to_all.36, f32[]{:T(128)} %broadcast.53), dimensions={1}, to_apply=%all_to_all.26.reduce_sub_computation | reduce | bytes 4325380 | tf_op jit(solution)/shard_map/all_to_all | solution.py:9
  67.3 12.4 %reshape.14 = f32[256,2,32,33]{3,2,1,0:T(8,128)} reshape(f32[16,33792]{1,0:T(8,128)S(1)} %reduce.6) | data formatting | bytes 4325376
  79.8 11.7 %copy.15 = f32[33,2,16,32,16]{3,2,4,1,0:T(8,128)} copy(f32[33,2,16,32,16]{0,3,1,4,2:T(8,128)} %bitcast.46) | data formatting | bytes 4325376 | tf_op jit(solution)/shard_map/all_to_all | solution.py:9
  91.5 6.7 %all_to_all.29 = f32[33,2,512,16]{2,3,1,0:T(8,128)S(1)} reshape(f32[33,2,16,32,16]{3,2,4,1,0:T(8,128)} %copy.15) | data formatting | bytes 4325376 | tf_op jit(solution)/shard_map/all_to_all | solution.py:9
  98.2 5.4 fusion.4
  103.5 0.0 all-reduce.2.cloned.1.call-update
  103.6 470.4 %all-reduce.2.cloned.1.call-done = f32[512,512]{1,0:T(8,128)} async-done(((f32[512,512]{1,0:T(8,128)}), f32[512,512]{1,0:T(8,128)}) %all-reduce.2.cloned.1.call-update) | async-done | bytes 1048592 | tf_op jit(solution)/shard_map/psum | solution.py:14
  574.0 0.0 copy-done
  574.0 2.4 fusion.13
  576.4 0.3 fusion.14
  576.6 0.1 copy.16
  576.7 5.8 cholesky.16
  582.6 0.7 compare_reduce_fusion
  583.3 0.7 fusion.10
  584.0 4.9 custom-call.7
  588.9 0.3 convolution_bitcast_fusion
  589.3 3.0 fusion.7
  592.3 1.0 copy.18
  593.3 1.0 reshape.15
  594.3 14.6 %all_to_all.37 = f32[16,1,4224]{2,1,0:T(1,128)S(1)} all-to-all(f32[16,1,4224]{2,1,0:T(1,128)S(1)} %reshape.15), channel_id=1, replica_groups=mesh['fib'=16,'blk'=32] {'fib'}, dimensions={0} | all-to-all | bytes 540672 | tf_op jit(solution)/shard_map/all_to_all | solution.py:20
  608.9 1.3 reduce.7
  610.2 1.1 reshape.16
  611.4 0.1 copy.20
  611.5 1.0 copy.21
  (2 shorter events, 0.0 us)
Async XLA Ops:
  6.5 567.5 %copy-start = (f32[512,64]{0,1:T(8,128)S(1)}, f32[512,64]{0,1:T(8,128)}, u32[]{:S(2)}) copy-start(f32[512,64]{0,1:T(8,128)} %param.3) | copy-start | bytes 393220
  6.5 567.5 %all-reduce.2.cloned.1.call-start = ((), (), s32[]{:S(2)}) async-start(), calls=%async_computation.2 | async-start | bytes 2097152 | tf_op jit(solution)/shard_map/psum | solution.py:14
Sparse Core Ops, SparseCore 0:
  103.7 470.2 all-reduce.1
where the time goes:
time: 620 us; the launch traced here: 619 us
  waiting for transfers between devices  470 us (76%)
  local copies, waits for them, and re-layouts  54.5 us (9%)
  blocking collectives  48.7 us (8%)
  other arithmetic  20.9 us (3%)
  between operations  13.5 us (2%)
  matrix products  11.3 us (2%)
    psum x1, waiting for transfers between devices, shards(): gram_total = lax.psum(local_gram, ('fib', 'blk'))  470 us
    all_to_all x1, blocking collectives, shards(): lax.all_to_all(field_data, 'fib', split_axis=3, concat_axis=2, tiled=True)  34.1 us
    unnamed x7, local copies, waits for them, and re-layouts  33.4 us
    all_to_all x3, local copies, waits for them, and re-layouts, shards(): lax.all_to_all(field_data, 'fib', split_axis=3, concat_axis=2, tiled=True)  18.9 us
    all_to_all x1, blocking collectives, shards(): lax.all_to_all(core_local, 'fib', split_axis=2, concat_axis=3, tiled=True)  14.6 us
  transfers between devices with their start and end apart: 1, of which 1 were waited for; matrix products, arithmetic and copies ran while one was open for 0% of the time, Pallas kernels for 0%

commit v1 on v0

--- a/solution.py
+++ b/solution.py
@@ -1,7 +1,19 @@
+import functools
 import jax
 import jax.numpy as jnp
 from jax import lax
 from jax.sharding import PartitionSpec as P
+
+
+def fill_flows(frame, mesh_dim):
+    opened = jnp.concatenate(
+        lax.all_to_all(jnp.stack(jnp.split(frame, lax.axis_size(mesh_dim), 2), 0), mesh_dim, 0, 0),
+        3,
+    )
+    return opened
+
+
+leaves_name = functools.partial(fill_flows, mesh_dim="fib")
 
 
 def shards(field_data, start_block):
@@ -17,7 +29,7 @@
     lower_factor = jnp.linalg.cholesky(inner_block)
     basis_cols = jax.scipy.linalg.solve_triangular(lower_factor, raw_basis.T, lower=True).T
     core_local = jnp.einsum("szxy,xr->szry", received, basis_cols, precision=highest)
-    return lax.all_to_all(core_local, "fib", split_axis=2, concat_axis=3, tiled=True)
+    return leaves_name(core_local)
 
 
 def solution(mesh):

time: 620 us -> 650 us (1.048)
  local copies, waits for them, and re-layouts: 54.5 us -> 83.3 us
    another operation x0 -> x18, local copies, waits for them, and re-layouts: none -> 29.5 us  [fill_flows(): jnp.stack(jnp.split(frame, lax.axis_size(mesh_dim), 2), 0)]
    unnamed x7 -> x44, local copies, waits for them, and re-layouts: 33.4 us -> 33.5 us
where the time goes in v1:
time: 650 us; the launch traced here: 649 us
  waiting for transfers between devices  471 us (72%)
  local copies, waits for them, and re-layouts  83.3 us (13%)
  blocking collectives  48.7 us (7%)
  other arithmetic  20.8 us (3%)
  between operations  13.8 us (2%)
  matrix products  11.3 us (2%)
    psum x1, waiting for transfers between devices, shards(): gram_total = lax.psum(local_gram, ('fib', 'blk'))  471 us
    all_to_all x1, blocking collectives, shards(): lax.all_to_all(field_data, 'fib', split_axis=3, concat_axis=2, tiled=True)  34.1 us
    unnamed x44, local copies, waits for them, and re-layouts  33.5 us
    another operation x18, local copies, waits for them, and re-layouts, fill_flows(): jnp.stack(jnp.split(frame, lax.axis_size(mesh_dim), 2), 0)  29.5 us
    all_to_all x3, local copies, waits for them, and re-layouts, shards(): lax.all_to_all(field_data, 'fib', split_axis=3, concat_axis=2, tiled=True)  19 us
    all_to_all x1, blocking collectives, fill_flows(): lax.all_to_all(jnp.stack(jnp.split(frame, lax.axis_size(mesh_dim), 2), 0)...  14.6 us
  transfers between devices with their start and end apart: 1, of which 1 were waited for; matrix products, arithmetic and copies ran while one was open for 0% of the time, Pallas kernels for 0%

profile of v1, /device:TPU:1, one launch (start us, length us, event | category | flops | bytes accessed | tf_op | source)
XLA Modules:
  0.0 648.6 jit_solution(9097699887688119448)
XLA Ops:
  6.5 8.7 %copy.11 = f32[33,2,32,256]{0,2,1,3:T(8,128)} copy(f32[33,2,32,256]{3,2,1,0:T(8,128)} %param.2) | data formatting | bytes 4325376 | tf_op args[0]
  15.2 10.1 %reshape.21 = f32[16,1,33792]{2,1,0:T(1,128)S(1)} reshape(f32[256,2,32,33]{3,2,1,0:T(8,128)} %bitcast.77) | data formatting | bytes 4325376
  25.3 34.1 %all_to_all.23 = f32[16,1,33792]{2,1,0:T(1,128)} all-to-all(f32[16,1,33792]{2,1,0:T(1,128)S(1)} %reshape.21), channel_id=1, replica_groups=mesh['fib'=16,'blk'=32] {'fib'}, dimensions={0} | all-to-all | bytes 4325376 | tf_op jit(solution)/shard_map/all_to_all | solution.py:21
  60.0 7.4 %reduce.6 = f32[16,33792]{1,0:T(8,128)S(1)} reduce(f32[16,1,33792]{2,1,0:T(1,128)} %all_to_all.23, f32[]{:T(128)} %broadcast.53), dimensions={1}, to_apply=%all_to_all.16.reduce_sub_computation | reduce | bytes 4325380 | tf_op jit(solution)/shard_map/all_to_all | solution.py:21
  67.4 12.4 %reshape.22 = f32[256,2,32,33]{3,2,1,0:T(8,128)} reshape(f32[16,33792]{1,0:T(8,128)S(1)} %reduce.6) | data formatting | bytes 4325376
  79.9 11.7 %copy.13 = f32[33,2,16,32,16]{3,2,4,1,0:T(8,128)} copy(f32[33,2,16,32,16]{0,3,1,4,2:T(8,128)} %bitcast.78) | data formatting | bytes 4325376 | tf_op jit(solution)/shard_map/all_to_all | solution.py:21
  91.6 6.7 %all_to_all.19 = f32[33,2,512,16]{2,3,1,0:T(8,128)S(1)} reshape(f32[33,2,16,32,16]{3,2,4,1,0:T(8,128)} %copy.13) | data formatting | bytes 4325376 | tf_op jit(solution)/shard_map/all_to_all | solution.py:21
  98.3 5.4 fusion.4
  103.7 470.7 %all-reduce.2.cloned.1.call-done = f32[512,512]{1,0:T(8,128)} async-done(((f32[512,512]{1,0:T(8,128)}), f32[512,512]{1,0:T(8,128)}) %all-reduce.2.cloned.1.call-update) | async-done | bytes 1048592 | tf_op jit(solution)/shard_map/psum | solution.py:26
  574.3 2.4 fusion.13
  577.0 5.8 cholesky.16
  584.2 4.9 custom-call.7
  589.5 3.0 fusion.7
  592.5 5.7 slice_bitcast_fusion
  598.2 1.4 copy.31
  599.6 1.4 copy.30
  601.0 2.0 copy.29
  603.0 2.0 copy.28
  605.0 2.0 copy.27
  607.1 2.0 copy.26
  609.1 2.0 copy.25
  611.1 2.0 copy.24
  613.1 2.0 copy.23
  615.2 2.0 copy.22
  617.2 2.0 copy.21
  619.2 0.9 copy.20
  620.2 0.9 copy.19
  622.5 1.0 reshape.23
  623.5 14.6 %all_to_all.24 = f32[16,1,4224]{2,1,0:T(1,128)S(1)} all-to-all(f32[16,1,4224]{2,1,0:T(1,128)S(1)} %reshape.23), channel_id=1, replica_groups=mesh['fib'=16,'blk'=32] {'fib'}, dimensions={0} | all-to-all | bytes 540672 | tf_op jit(solution)/shard_map/all_to_all | solution.py:10
  638.1 1.3 reduce.7
  639.4 1.1 reshape.24
  640.7 1.0 copy.33
  (55 shorter events, 3.9 us)
Async XLA Ops:
  6.5 567.8 %copy-start = (f32[512,64]{0,1:T(8,128)S(1)}, f32[512,64]{0,1:T(8,128)}, u32[]{:S(2)}) copy-start(f32[512,64]{0,1:T(8,128)} %param.3) | copy-start | bytes 393220
  6.5 567.8 %all-reduce.2.cloned.1.call-start = ((), (), s32[]{:S(2)}) async-start(), calls=%async_computation.2 | async-start | bytes 2097152 | tf_op jit(solution)/shard_map/psum | solution.py:26
  620.1 2.0 copy-start.10
  620.1 2.1 copy-start.9
  620.1 2.1 copy-start.8
  620.1 2.1 copy-start.7
  620.1 2.1 copy-start.6
  620.1 2.1 copy-start.5
  620.2 2.2 copy-start.4
  620.2 2.2 copy-start.3
  620.2 2.2 copy-start.2
  620.2 2.2 copy-start.1
  621.1 1.0 copy-start.11
Sparse Core Ops, SparseCore 0:
  103.8 470.5 all-reduce.1
